TPU v7x, 512 devices: a whole 4x8x8 slice. The times are simulated.
512 devices in a mesh: seq: 8 (over y_lo, x), fsdp: 64 (over z, y_hi, core).
Axes of the slice: x: 4, y: 8 (y_hi: 4, y_lo: 2; y = y_hi * 2 + y_lo), z: 8, core: 2. Of those that a mesh axis runs over, the one named last changes fastest.
Arguments:
- hidden: bfloat16 [2048, 8192], P('seq', 'fsdp'), may hold values from -28 to 28
- q_weight: bfloat16 [8192, 8192], P('fsdp'), may hold values from -0.0625 to 0.0625
- kv_weight: bfloat16 [2048, 8192], P(None, 'fsdp'), may hold values from -0.0625 to 0.0625
- d_attended: bfloat16 [2048, 8192], P('seq', 'fsdp'), may hold values from -6 to 6
- doc_lengths: int32 [4], replicated, may hold values from 1 to 1536, as said below
- prompt_pos: int32 [128], replicated, may hold values from 0 to 2047, as said below
Outputs:
- attended: bfloat16 [2048, 8192], P('seq', 'fsdp')
- prompt_grad: float32 [128, 8192], P('seq', 'fsdp')
Inputs may be any that keep to these rules, and one draw needn't show every extreme that they name: `doc_lengths`: 4 document lengths in pack order that sum to 2048; exactly one is 1536, at a position that varies from draw to draw, and the others are at least 1. `prompt_pos`: for every block i of 256 rows, entries i * 16 to (i + 1) * 16 - 1 are distinct rows of that block in rising order; row 0 and row 2047 are always among them.
All inputs are finite; a program needn't handle non-finite values.
Results may differ from a plain program's by a relative error of at most 0.017.
The roundings to bfloat16 on the way count: a program that leaves them out, or rounds other values in their place, can miss the bound.
Values may be sent and summed in bfloat16 or wider, within the bound.
A program may use at most 64 MiB of HBM per device.

v0:
```python
import math
import jax
import jax.numpy as jnp
from jax import lax
from jax.sharding import PartitionSpec as P

GROUP = 8
rope_theta = 1000000.0


def locate(tokens, doc_lengths):
    doc_ends = jnp.cumsum(doc_lengths)
    segment = jnp.sum((tokens[:, None] >= doc_ends[None, :]).astype(jnp.int32), axis=1)
    doc_starts = doc_ends - doc_lengths
    picked = segment[:, None] == jnp.arange(doc_lengths.shape[0], dtype=jnp.int32)[None, :]
    opening = jnp.sum(jnp.where(picked, doc_starts[None, :], 0), axis=1)
    return (segment, tokens - opening)


def rotate(vectors, positions, factor):
    halfway = vectors.shape[-1] // 2
    steps_up = jnp.arange(halfway, dtype=jnp.float32)
    frequency = jnp.exp(steps_up * (-2.0 * math.log(rope_theta) / vectors.shape[-1]))
    angles = positions.astype(jnp.float32)[:, None] * frequency[None, :]
    cosine = jnp.cos(angles)
    sine_part = jnp.sin(angles)
    leading = vectors[..., :halfway]
    trailing = vectors[..., halfway:]
    return jnp.concatenate(
        [
            leading * cosine - factor * trailing * sine_part,
            trailing * cosine + factor * leading * sine_part,
        ],
        axis=-1,
    )


def per_device(hidden, q_weight, kv_weight, d_attended, doc_lengths, prompt_pos):
    seq_count = lax.axis_size("seq")
    row_count = hidden.shape[0]
    head_dim = q_weight.shape[0]
    kv_width = kv_weight.shape[0]
    seq_length = row_count * seq_count
    prompt_count = prompt_pos.shape[0]
    prompt_local = prompt_count // seq_count
    seq_rank = lax.axis_index("seq")
    fsdp_rank = lax.axis_index("fsdp")
    group_index = fsdp_rank // GROUP
    score_scale = 1.0 / math.sqrt(head_dim)
    first_row = seq_rank * row_count
    all_tokens = jnp.arange(seq_length, dtype=jnp.int32)
    segment_all, place_all = locate(all_tokens, doc_lengths)
    own_tokens = first_row + jnp.arange(row_count, dtype=jnp.int32)
    segment_own = lax.dynamic_slice_in_dim(segment_all, first_row, row_count)
    place_own = lax.dynamic_slice_in_dim(place_all, first_row, row_count)
    kv_partial = lax.dot_general(
        hidden, kv_weight, (((1,), (1,)), ((), ())), preferred_element_type=jnp.float32
    )
    kv_summed = lax.psum(kv_partial, "fsdp")
    kv_group = lax.dynamic_slice_in_dim(
        kv_summed, group_index * 2 * head_dim, 2 * head_dim, 1
    ).astype(jnp.bfloat16)
    key_own = rotate(kv_group[:, :head_dim].astype(jnp.float32), place_own, 1.0).astype(
        jnp.bfloat16
    )
    kv_block = jnp.concatenate([key_own, kv_group[:, head_dim:]], axis=1)
    kv_full = lax.all_gather(kv_block, "seq", axis=0, tiled=True)
    q_pre = lax.dot_general(
        lax.all_gather(hidden, "fsdp", axis=1, tiled=True),
        q_weight,
        (((1,), (1,)), ((), ())),
        preferred_element_type=jnp.float32,
    )
    own_query = rotate(q_pre, place_own, 1.0).astype(jnp.bfloat16)
    block_len = 512
    block_count = seq_length // block_len
    key_blocks = kv_full[:, :head_dim].reshape(block_count, block_len, head_dim)
    value_blocks = kv_full[:, head_dim:].reshape(block_count, block_len, head_dim)
    key_segments = segment_all.reshape(block_count, block_len)
    key_tokens = all_tokens.reshape(block_count, block_len)
    raw_scores = (
        jnp.einsum("tc,bkc->btk", own_query, key_blocks, preferred_element_type=jnp.float32)
        * score_scale
    )
    allowed = (key_segments[:, None, :] == segment_own[None, :, None]) & (
        key_tokens[:, None, :] <= own_tokens[None, :, None]
    )
    scores = jnp.where(allowed, raw_scores, -jnp.inf)
    row_max = jnp.max(scores, axis=(0, 2))
    exponent_terms = jnp.exp(scores - row_max[None, :, None])
    row_sum = jnp.sum(exponent_terms, axis=(0, 2))
    attention_probs = (exponent_terms / row_sum[None, :, None]).astype(jnp.bfloat16)
    attended_sum = jnp.einsum(
        "btk,bkc->tc", attention_probs, value_blocks, preferred_element_type=jnp.float32
    )
    attended = attended_sum.astype(jnp.bfloat16)
    rowdot = jnp.sum(d_attended.astype(jnp.float32) * attended.astype(jnp.float32), axis=1)
    local_prompts = (
        lax.dynamic_slice_in_dim(prompt_pos, seq_rank * prompt_local, prompt_local) - first_row
    )
    row_probs = jnp.take(attention_probs, local_prompts, axis=1)
    row_upstream = jnp.take(d_attended, local_prompts, axis=0)
    row_dprobs = jnp.einsum(
        "pc,bkc->bpk", row_upstream, value_blocks, preferred_element_type=jnp.float32
    )
    row_dot = jnp.take(rowdot, local_prompts)
    row_dscores = (row_probs.astype(jnp.float32) * (row_dprobs - row_dot[None, :, None])).astype(
        jnp.bfloat16
    )
    query_grad = (
        jnp.einsum("bpk,bkc->pc", row_dscores, key_blocks, preferred_element_type=jnp.float32)
        * score_scale
    )
    query_grad = rotate(query_grad, jnp.take(place_own, local_prompts), -1.0).astype(jnp.bfloat16)
    block_of = prompt_pos // block_len
    column_of = prompt_pos % block_len
    col_probs = attention_probs[block_of, :, column_of]
    col_values = value_blocks[block_of, column_of]
    col_dprobs = lax.dot_general(
        col_values, d_attended, (((1,), (1,)), ((), ())), preferred_element_type=jnp.float32
    )
    col_dscores = (col_probs.astype(jnp.float32) * (col_dprobs - rowdot[None, :])).astype(
        jnp.bfloat16
    )
    key_grad = jnp.dot(col_dscores, own_query, preferred_element_type=jnp.float32) * score_scale
    key_grad = rotate(key_grad, jnp.take(place_all, prompt_pos), -1.0)
    value_grad = jnp.dot(col_probs, d_attended, preferred_element_type=jnp.float32)
    kv_grad_mine = jnp.concatenate([key_grad, value_grad], axis=1)
    seq_summed = lax.psum_scatter(kv_grad_mine, "seq", scatter_dimension=0, tiled=True)
    wide_own = jnp.zeros((prompt_local, kv_width), jnp.float32)
    wide_own = lax.dynamic_update_slice_in_dim(wide_own, seq_summed, group_index * 2 * head_dim, 1)
    kv_grad = lax.psum(wide_own, "fsdp").astype(jnp.bfloat16)
    q_part = lax.psum_scatter(
        lax.dot_general(
            q_weight, query_grad, (((0,), (1,)), ((), ())), preferred_element_type=jnp.float32
        ),
        "fsdp",
        scatter_dimension=0,
        tiled=True,
    )
    kv_part = jnp.dot(kv_grad, kv_weight, preferred_element_type=jnp.float32)
    prompt_grad = q_part.T + kv_part
    return (attended, prompt_grad)


def solution(mesh):
    placed = (P("seq", "fsdp"), P("fsdp", None), P(None, "fsdp"), P("seq", "fsdp"), P(), P())
    return jax.shard_map(
        per_device,
        mesh=mesh,
        in_specs=placed,
        out_specs=(P("seq", "fsdp"), P("seq", "fsdp")),
        check_vma=False,
    )
```

profile of v0, /device:TPU:8, one launch (start us, length us, event | category | flops | bytes accessed | tf_op | source)
XLA Modules:
  0.0 729.2 jit_solution(16325572370149899096)
XLA Ops:
  7.2 0.7 all-gather.5.cloned.1.call-update
  8.0 2.8 fusion.74
  11.3 314.8 %all-reduce.2 = bf16[256,2048]{0,1:T(8,128)(2,1)S(1)} all-reduce(f32[256,2048]{0,1:T(8,128)} %fusion.74), channel_id=1, replica_groups=mesh['seq'=8,'fsdp'=64] {'fsdp'}, use_global_device_ids=true, to_apply=%region_2.3 | all-reduce | flops 524288 | bytes 3145728 | tf_op jit(solution)/shard_map/psum | solution.py:59
  326.2 3.7 fusion.75
  330.3 0.7 pad_maximum_fusion
  331.2 0.6 compare_and_fusion
  331.9 0.6 gather_fusion.1
  332.4 0.7 gather_fusion.3
  333.1 1.1 gather_fusion.6
  334.3 0.5 select_convert_fusion
  334.8 0.5 fusion.65
  335.3 36.3 %all-gather.3.cloned.1.call-done = bf16[2048,256]{0,1:T(8,128)(2,1)} async-done(((bf16[256,256]{0,1:T(8,128)(2,1)}), bf16[2048,256]{0,1:T(8,128)(2,1)}) %all-gather.3.cloned.1.call-update) | async-done | bytes 1048592 | tf_op jit(solution)/shard_map/all_gather | solution.py:67
  371.7 2.1 fusion.72
  374.1 0.7 fusion.73
  375.6 1.8 copy.48
  377.4 1.8 gather_fusion
  379.2 2.0 copy.62
  381.3 1.1 gather_fusion.4
  382.4 2.5 gather_fusion.5
  384.9 1.4 multiply_reduce_fusion
  386.4 0.7 gather_fusion.2
  387.0 0.6 broadcast_select_fusion
  387.9 1.1 convolution_multiply_fusion
  389.0 0.9 fusion.38
  389.9 0.8 copy.59
  390.7 1.6 fusion.9
  392.4 1.2 convolution_bitcast_fusion
  393.7 0.7 copy.54
  394.4 39.2 %reduce-scatter.7.cloned.1.call-done = f32[16,256]{1,0:T(8,128)} async-done(((f32[128,256]{1,0:T(8,128)}), f32[16,256]{1,0:T(8,128)}) %reduce-scatter.7.cloned.1.call-update) | async-done | bytes 16400
  433.6 0.8 copy.60
  434.6 286.0 %all-reduce.3 = bf16[16,2048]{0,1:T(8,128)(2,1)} all-reduce(f32[16,2048]{0,1:T(8,128)S(1)} %constant_dynamic-update-slice_fusion), channel_id=1, replica_groups=mesh['seq'=8,'fsdp'=64] {'fsdp'}, use_global_device_ids=true, to_apply=%region_9.10 | all-reduce | flops 32768 | bytes 196608 | tf_op jit(solution)/shard_map/psum | solution.py:132
  720.5 2.1 convolution_add_fusion
  (49 shorter events, 2.9 us)
Async XLA Ops:
  7.2 319.1 %copy-start = (bf16[128,8192]{1,0:T(8,128)(2,1)S(1)}, bf16[128,8192]{1,0:T(8,128)(2,1)}, u32[]{:S(2)}) copy-start(bf16[128,8192]{1,0:T(8,128)(2,1)} %param.7) | copy-start | bytes 6291460
  7.2 3.7 copy-start.6
  7.2 319.0 %all-gather.5.cloned.1.call-start = ((), (), s32[]{:S(2)}) async-start(), calls=%async_computation.3 | async-start | bytes 4259840 | tf_op jit(solution)/shard_map/all_gather | solution.py:69
  7.9 363.7 %all-gather.3.cloned.1.call-start = ((), (), s32[]{:S(2)}) async-start(), calls=%async_computation.2 | async-start | bytes 1179648 | tf_op jit(solution)/shard_map/all_gather | solution.py:67
  326.2 5.0 copy-start.2
  326.2 5.1 copy-start.4
  331.0 102.7 %reduce-scatter.7.cloned.1.call-start = ((), (), s32[]{:S(2)}) async-start(), calls=%async_computation.5 | async-start | bytes 147456
  331.9 42.2 %copy-start.3 = (s32[16]{0:T(128)}, s32[16]{0:T(128)S(1)}, u32[]{:S(2)}) copy-start(s32[16]{0:T(128)S(1)} %get-tuple-element.13) | copy-start | bytes 196
  374.1 0.8 copy-start.1
  386.4 5.9 copy-start.5
  390.6 329.9 %reduce-scatter.5.cloned.1.call-start = ((), (), s32[]{:S(2)}) async-start(), calls=%async_computation.4 | async-start | bytes 532480 | tf_op jit(solution)/shard_map/reduce_scatter | solution.py:133
Sparse Core Ops, SparseCore 0:
  11.2 95.6 all-gather.4
  331.1 40.5 all-gather.2
  390.7 42.8 reduce-scatter.6
  438.0 139.4 reduce-scatter.4
where the time goes:
time: 730 us; the launch traced here: 729 us
  blocking collectives  601 us (82%)
  waiting for transfers between devices  76.3 us (10%)
  local copies, waits for them, and re-layouts  17.6 us (2%)
  matrix products  14.9 us (2%)
  between operations  14 us (2%)
    psum x1, blocking collectives, per_device(): kv_summed = lax.psum(kv_partial, 'fsdp')  315 us
    psum x1, blocking collectives, per_device(): kv_grad = lax.psum(wide_own, 'fsdp').astype(jnp.bfloat16)  286 us
    unnamed x5, waiting for transfers between devices  39.9 us
    all_gather x1, waiting for transfers between devices, per_device(): kv_full = lax.all_gather(kv_block, 'seq', axis=0, tiled=True)  36.3 us
  transfers between devices with their start and end apart: 4, of which 2 were waited for; matrix products, arithmetic and copies ran while one was open for 2% of the time, Pallas kernels for 0%

commit v1 on v0

--- a/solution.py
+++ b/solution.py
@@ -129,7 +129,11 @@
     seq_summed = lax.psum_scatter(kv_grad_mine, "seq", scatter_dimension=0, tiled=True)
     wide_own = jnp.zeros((prompt_local, kv_width), jnp.float32)
     wide_own = lax.dynamic_update_slice_in_dim(wide_own, seq_summed, group_index * 2 * head_dim, 1)
-    kv_grad = lax.psum(wide_own, "fsdp").astype(jnp.bfloat16)
+
+    def define_the_loads(x0):
+        return lax.all_gather(x0, "fsdp").sum(axis=0)
+
+    kv_grad = define_the_loads(wide_own).astype(jnp.bfloat16)
     q_part = lax.psum_scatter(
         lax.dot_general(
             q_weight, query_grad, (((0,), (1,)), ((), ())), preferred_element_type=jnp.float32

time: 730 us -> 684 us (0.937)
  the two profiles are of different devices: /device:TPU:8 before, /device:TPU:2 now
where the time goes in v1:
time: 684 us; the launch traced here: 683 us
  waiting for transfers between devices  317 us (46%)
  blocking collectives  311 us (45%)
  local copies, waits for them, and re-layouts  18.4 us (3%)
  matrix products  14.4 us (2%)
  between operations  14.1 us (2%)
  other arithmetic  7.73 us (1%)
    psum x1, blocking collectives, per_device(): kv_summed = lax.psum(kv_partial, 'fsdp')  311 us
    reduce_scatter x1, waiting for transfers between devices, per_device(): lax.psum_scatter(lax.dot_general(q_weight, query_grad, (((0,), (1,)), (()...  136 us
    all_gather x1, waiting for transfers between devices, define_the_loads(): return lax.all_gather(x0, 'fsdp').sum(axis=0)  96.3 us
    unnamed x6, waiting for transfers between devices  43.1 us
    all_gather x1, waiting for transfers between devices, per_device(): kv_full = lax.all_gather(kv_block, 'seq', axis=0, tiled=True)  41.5 us
  transfers between devices with their start and end apart: 5, of which 4 were waited for; matrix products, arithmetic and copies ran while one was open for 3% of the time, Pallas kernels for 0%

profile of v1, /device:TPU:2, one launch (start us, length us, event | category | flops | bytes accessed | tf_op | source)
XLA Modules:
  0.0 683.1 jit_solution(801676571477464284)
XLA Ops:
  7.2 0.7 all-gather.6.cloned.1.call-update
  8.0 0.8 reduce-window.8
  8.8 2.8 fusion.74
  12.0 311.1 %all-reduce.1 = bf16[256,2048]{0,1:T(8,128)(2,1)S(1)} all-reduce(f32[256,2048]{0,1:T(8,128)} %fusion.74), channel_id=1, replica_groups=mesh['seq'=8,'fsdp'=64] {'fsdp'}, use_global_device_ids=true, to_apply=%region_2.3 | all-reduce | flops 524288 | bytes 3145728 | tf_op jit(solution)/shard_map/psum | solution.py:59
  323.2 3.7 fusion.75
  327.3 0.7 pad_maximum_fusion
  328.1 1.1 gather_fusion.6
  329.4 41.5 %all-gather.4.cloned.1.call-done = bf16[2048,256]{0,1:T(8,128)(2,1)} async-done(((bf16[256,256]{0,1:T(8,128)(2,1)}), bf16[2048,256]{0,1:T(8,128)(2,1)}) %all-gather.4.cloned.1.call-update) | async-done | bytes 1048592 | tf_op jit(solution)/shard_map/all_gather | solution.py:67
  370.9 2.1 fusion.72
  373.0 1.3 copy.63
  374.3 1.0 copy.65
  375.3 0.7 fusion.73
  376.7 2.6 gather_fusion.5
  379.2 1.1 gather_fusion.4
  380.3 1.4 multiply_reduce_fusion
  382.0 1.1 convolution_multiply_fusion
  383.3 0.7 copy.61
  384.2 42.4 %reduce-scatter.7.cloned.1.call-done = f32[16,256]{1,0:T(8,128)} async-done(((f32[128,256]{1,0:T(8,128)}), f32[16,256]{1,0:T(8,128)}) %reduce-scatter.7.cloned.1.call-update) | async-done | bytes 16400
  426.5 0.8 copy.62
  427.5 0.7 copy-done.4
  428.2 0.7 compare_and_fusion
  429.5 0.7 gather_fusion.3
  430.2 0.7 gather_fusion.2
  430.9 1.9 copy.48
  432.7 1.8 gather_fusion
  434.6 1.6 fusion.9
  436.3 1.3 convolution_bitcast_fusion
  437.6 0.7 copy.56
  438.4 96.3 %all-gather.8.cloned.1.call-done = f32[64,16,2048]{2,1,0:T(8,128)} async-done(((f32[1,16,2048]{2,1,0:T(8,128)}), f32[64,16,2048]{2,1,0:T(8,128)}) %all-gather.8.cloned.1.call-update) | async-done | bytes 8388624 | tf_op jit(solution)/shard_map/all_gather | solution.py:134
  534.6 3.8 reduce_sum.49
  538.7 136.3 %reduce-scatter.5.cloned.1.call-done = f32[128,16]{0,1:T(8,128)} async-done(((f32[8192,16]{0,1:T(8,128)}), f32[128,16]{0,1:T(8,128)}) %reduce-scatter.5.cloned.1.call-update) | async-done | bytes 8208 | tf_op jit(solution)/shard_map/reduce_scatter | solution.py:137
  675.0 1.6 convolution_add_fusion
  (54 shorter events, 3.4 us)
Async XLA Ops:
  7.2 316.0 %copy-start = (bf16[128,8192]{1,0:T(8,128)(2,1)S(1)}, bf16[128,8192]{1,0:T(8,128)(2,1)}, u32[]{:S(2)}) copy-start(bf16[128,8192]{1,0:T(8,128)(2,1)} %param.7) | copy-start | bytes 6291460
  7.2 4.6 copy-start.6
  7.2 316.0 %all-gather.6.cloned.1.call-start = ((), (), s32[]{:S(2)}) async-start(), calls=%async_computation.3 | async-start | bytes 4259840 | tf_op jit(solution)/shard_map/all_gather | solution.py:69
  7.9 363.0 %all-gather.4.cloned.1.call-start = ((), (), s32[]{:S(2)}) async-start(), calls=%async_computation.2 | async-start | bytes 1179648 | tf_op jit(solution)/shard_map/all_gather | solution.py:67
  323.2 5.0 copy-start.5
  323.2 6.1 copy-start.3
  328.0 98.6 %reduce-scatter.7.cloned.1.call-start = ((), (), s32[]{:S(2)}) async-start(), calls=%async_computation.6 | async-start | bytes 147456
  374.3 1.7 copy-start.1
  384.1 150.5 %all-gather.8.cloned.1.call-start = ((), (), s32[]{:S(2)}) async-start(), calls=%async_computation.5 | async-start | bytes 8519680 | tf_op jit(solution)/shard_map/all_gather | solution.py:134
  427.4 0.7 copy-start.4
  428.1 246.8 %reduce-scatter.5.cloned.1.call-start = ((), (), s32[]{:S(2)}) async-start(), calls=%async_computation.4 | async-start | bytes 532480 | tf_op jit(solution)/shard_map/reduce_scatter | solution.py:137
  438.4 236.6 %copy-start.2 = (bf16[2048,128]{1,0:T(8,128)(2,1)S(1)}, bf16[2048,128]{1,0:T(8,128)(2,1)}, u32[]{:S(2)}) copy-start(bf16[2048,128]{1,0:T(8,128)(2,1)} %param.8) | copy-start | bytes 1572868
Sparse Core Ops, SparseCore 0:
  11.2 92.9 all-gather.5
  328.1 42.7 all-gather.3
  384.2 42.2 reduce-scatter.6
  429.7 104.8 all-gather.7
  538.9 135.9 reduce-scatter.4

commit v2 on v0

--- a/solution.py
+++ b/solution.py
@@ -3,6 +3,7 @@
 import jax.numpy as jnp
 from jax import lax
 from jax.sharding import PartitionSpec as P
+from jax.lax import all_to_all, axis_size
 
 GROUP = 8
 rope_theta = 1000000.0
@@ -64,7 +65,11 @@
         jnp.bfloat16
     )
     kv_block = jnp.concatenate([key_own, kv_group[:, head_dim:]], axis=1)
-    kv_full = lax.all_gather(kv_block, "seq", axis=0, tiled=True)
+    vec_out = tuple((kv_block for _ in range(axis_size("seq"))))
+    parts_out = jnp.stack(vec_out, 0)
+    kv_full = jnp.concatenate(
+        all_to_all(parts_out, concat_axis=0, split_axis=0, axis_name="seq"), 0
+    )
     q_pre = lax.dot_general(
         lax.all_gather(hidden, "fsdp", axis=1, tiled=True),
         q_weight,

time: 730 us -> 695 us (0.952)
  waiting for transfers between devices: 76.3 us -> 38.9 us
  starting transfers between devices: 0.16 us -> 9.14 us
    all_gather x1 -> x0, waiting for transfers between devices: 36.3 us -> none  [per_device(): kv_full = lax.all_gather(kv_block, 'seq', axis=0, tiled=True)]
    all_to_all x0 -> x1, starting transfers between devices: none -> 9.06 us  [per_device(): all_to_all(parts_out, concat_axis=0, split_axis=0, axis_name='seq')]
    unnamed x5 -> x4, waiting for transfers between devices: 39.9 us -> 33.1 us
where the time goes in v2:
time: 695 us
  blocking collectives  598 us (86%)
  waiting for transfers between devices  38.9 us (6%)
  local copies, waits for them, and re-layouts  15.3 us (2%)
  matrix products  14.9 us (2%)
  between operations  14 us (2%)
  starting transfers between devices  9.14 us (1%)
    psum x1, blocking collectives, per_device(): kv_summed = lax.psum(kv_partial, 'fsdp')  312 us
    psum x1, blocking collectives, per_device(): kv_grad = lax.psum(wide_own, 'fsdp').astype(jnp.bfloat16)  286 us
    unnamed x4, waiting for transfers between devices  33.1 us
  transfers between devices with their start and end apart: 4, of which 2 were waited for; matrix products, arithmetic and copies ran while one was open for 2% of the time, Pallas kernels for 0%

profile of v2, /device:TPU:8, one launch (start us, length us, event | category | flops | bytes accessed | tf_op | source)
XLA Modules:
  0.0 694.8 jit_solution(8466334145542350254)
XLA Ops:
  7.2 0.7 all-gather.2.cloned.1.call-update
  7.9 2.8 fusion.74
  11.3 311.5 %all-reduce.2 = bf16[256,2048]{0,1:T(8,128)(2,1)S(1)} all-reduce(f32[256,2048]{0,1:T(8,128)} %fusion.74), channel_id=1, replica_groups=mesh['seq'=8,'fsdp'=64] {'fsdp'}, use_global_device_ids=true, to_apply=%region_2.3 | all-reduce | flops 524288 | bytes 3145728 | tf_op jit(solution)/shard_map/psum | solution.py:60
  322.9 3.7 fusion.75
  327.1 1.0 stack.2
  328.1 9.1 %all-to-all-start = ((bf16[8,256,256]{2,1,0:T(8,128)(2,1)}), bf16[8,256,256]{2,1,0:T(8,128)(2,1)S(1)}, u32[]{:S(2)}, u32[]{:S(2)}) async-start(bf16[8,256,256]{2,1,0:T(8,128)(2,1)} %stack.2), calls=%async_computation | async-start | bytes 2097152 | tf_op jit(solution)/shard_map/all_to_all | solution.py:71
  337.4 0.6 compare_and_fusion
  338.1 0.6 gather_fusion.1
  338.7 0.7 gather_fusion.3
  339.3 1.1 gather_fusion.6
  340.5 0.5 select_convert_fusion
  341.0 0.5 fusion.65
  341.5 5.7 all-to-all-done
  347.3 0.9 fusion.72
  348.1 0.7 fusion.73
  349.6 1.8 copy.48
  351.4 1.8 gather_fusion
  353.3 1.1 gather_fusion.4
  354.4 2.6 gather_fusion.5
  356.9 1.4 multiply_reduce_fusion
  358.4 0.8 gather_fusion.2
  359.2 0.6 broadcast_select_fusion
  360.0 1.1 convolution_multiply_fusion
  361.1 0.8 fusion.38
  361.9 0.7 copy.57
  362.7 1.6 fusion.9
  364.5 1.2 convolution_bitcast_fusion
  365.8 0.7 copy.51
  366.5 32.4 %reduce-scatter.7.cloned.1.call-done = f32[16,256]{1,0:T(8,128)} async-done(((f32[128,256]{1,0:T(8,128)}), f32[16,256]{1,0:T(8,128)}) %reduce-scatter.7.cloned.1.call-update) | async-done | bytes 16400
  398.9 0.8 copy.58
  399.8 286.3 %all-reduce.3 = bf16[16,2048]{0,1:T(8,128)(2,1)} all-reduce(f32[16,2048]{0,1:T(8,128)S(1)} %constant_dynamic-update-slice_fusion), channel_id=1, replica_groups=mesh['seq'=8,'fsdp'=64] {'fsdp'}, use_global_device_ids=true, to_apply=%region_9.10 | all-reduce | flops 32768 | bytes 196608 | tf_op jit(solution)/shard_map/psum | solution.py:137
  686.1 2.1 convolution_add_fusion
  (56 shorter events, 2.6 us)
Async XLA Ops:
  7.2 315.7 %copy-start = (bf16[128,8192]{1,0:T(8,128)(2,1)S(1)}, bf16[128,8192]{1,0:T(8,128)(2,1)}, u32[]{:S(2)}) copy-start(bf16[128,8192]{1,0:T(8,128)(2,1)} %param.7) | copy-start | bytes 6291460
  7.2 3.6 copy-start.10
  7.2 315.7 %all-gather.2.cloned.1.call-start = ((), (), s32[]{:S(2)}) async-start(), calls=%async_computation.3 | async-start | bytes 4259840 | tf_op jit(solution)/shard_map/all_gather | solution.py:74
  11.0 315.6 %copy-start.4 = (f32[64]{0:T(128)}, f32[64]{0:T(128)S(1)}, u32[]{:S(2)}) copy-start(f32[64]{0:T(128)S(1)} %multiply_exponential_fusion) | copy-start | bytes 772
  326.6 10.7 %copy-start.2 = (bf16[256,128]{1,0:T(8,128)(2,1)S(1)}, bf16[256,128]{1,0:T(8,128)(2,1)}, u32[]{:S(2)}) copy-start(bf16[256,128]{1,0:T(8,128)(2,1)} %param.9) | copy-start | bytes 196612
  326.6 10.8 %copy-start.8 = (s32[128]{0:T(128)S(1)}, s32[128]{0:T(128)}, u32[]{:S(2)}) copy-start(s32[128]{0:T(128)} %param.11) | copy-start | bytes 1540
  328.1 19.1 %all-to-all-start = ((bf16[8,256,256]{2,1,0:T(8,128)(2,1)}), bf16[8,256,256]{2,1,0:T(8,128)(2,1)S(1)}, u32[]{:S(2)}, u32[]{:S(2)}) async-start(bf16[8,256,256]{2,1,0:T(8,128)(2,1)} %stack.2), calls=%async_computation | async-start | bytes 2097152 | tf_op jit(solution)/shard_map/all_to_all | solution.py:71
  337.2 61.7 %reduce-scatter.7.cloned.1.call-start = ((), (), s32[]{:S(2)}) async-start(), calls=%async_computation.5 | async-start | bytes 147456
  338.1 10.7 %copy-start.7 = (s32[16]{0:T(128)}, s32[16]{0:T(128)S(1)}, u32[]{:S(2)}) copy-start(s32[16]{0:T(128)S(1)} %get-tuple-element.13) | copy-start | bytes 196
  338.1 13.3 %copy-start.3 = (s32[1024]{0:T(1024)}, s32[1024]{0:T(1024)S(1)}, u32[]{:S(2)}) copy-start(s32[1024]{0:T(1024)S(1)} %pad_clamp_fusion.1) | copy-start | bytes 12292
  348.1 0.8 copy-start.1
  351.4 9.7 %copy-start.5 = (f32[64]{0:T(128)S(1)}, f32[64]{0:T(128)}, u32[]{:S(2)}) copy-start(f32[64]{0:T(128)} %copy-done.4) | copy-start | bytes 772
  354.4 8.4 %copy-start.6 = (pred[16]{0:T(512)(128)(4,1)S(1)}, pred[16]{0:T(512)(128)(4,1)}, u32[]{:S(2)}) copy-start(pred[16]{0:T(512)(128)(4,1)} %get-tuple-element.12) | copy-start | bytes 52
  358.4 6.0 copy-start.9
  362.7 323.5 %reduce-scatter.5.cloned.1.call-start = ((), (), s32[]{:S(2)}) async-start(), calls=%async_computation.4 | async-start | bytes 532480 | tf_op jit(solution)/shard_map/reduce_scatter | solution.py:138
Sparse Core Ops, SparseCore 0:
  11.2 94.1 all-gather.1
  362.8 36.0 reduce-scatter.6
  403.4 139.4 reduce-scatter.4
